TPU v7x, 256 devices: a whole 4x4x8 slice. The times are simulated.
256 devices in a mesh: inner: 32 (over z, y_hi, core), outer: 8 (over y_lo, x).
Axes of the slice: x: 4, y: 4 (y_hi: 2, y_lo: 2; y = y_hi * 2 + y_lo), z: 8, core: 2. Of those that a mesh axis runs over, the one named last changes fastest.
Arguments:
- queries: bfloat16 [32768, 1024], P(('outer', 'inner')), may hold values from -8 to 8
- key_rows: bfloat16 [32768, 128], P(('outer', 'inner')), may hold values from -8 to 8
- value_rows: bfloat16 [32768, 128], P(('outer', 'inner')), may hold values from -6 to 6
- grad_output: bfloat16 [32768, 1024], P(('outer', 'inner')), may hold values from -6 to 6
- doc_blocks: int32 [256], replicated, may hold values from 0 to 31, never falling along the last dimension, each value on 1 to 32 neighbouring positions
Outputs:
- grad_queries: bfloat16 [32768, 1024], P(('outer', 'inner'))
- grad_keys: bfloat16 [32768, 128], P(('outer', 'inner'))
- grad_values: bfloat16 [32768, 128], P(('outer', 'inner'))
All inputs are finite; a program needn't handle non-finite values.
Results may differ from a plain program's by a relative error of at most 0.019.
Values may be sent and summed in bfloat16 or wider, within the bound.
A program may use at most 64 MiB of HBM per device.

v0:
```python
import jax
import jax.numpy as jnp
from jax import lax
from jax.sharding import PartitionSpec as P


def shifted(block, axis, distance):
    devices = range(lax.axis_size(axis))
    route = [(i - distance, i) for i in devices if i - distance in devices]
    return lax.ppermute(block, axis, route)


def shards(queries, key_rows, value_rows, grad_output, doc_blocks):
    token_count = queries.shape[0]
    width = key_rows.shape[1]
    head_count = queries.shape[1] // width
    inner_count = lax.axis_size("inner")
    outer_count = lax.axis_size("outer")
    inner_at = lax.axis_index("inner")
    outer_at = lax.axis_index("outer")
    blocks_dev = doc_blocks.shape[0] // (inner_count * outer_count)
    block_len = token_count // blocks_dev
    tile_blocks = 4
    span_blocks = inner_count * blocks_dev
    win_blocks = -(-(span_blocks + blocks_dev) // tile_blocks) * tile_blocks
    pad_blocks = max(0, (inner_count - 1) * blocks_dev + win_blocks - 2 * span_blocks)
    tile_count = win_blocks // tile_blocks
    tile_len = tile_blocks * block_len
    scaling = width ** (-0.5)
    earlier_k, earlier_v = shifted((key_rows, value_rows), "outer", 1)
    group_k, group_v, prior_k, prior_v = (
        lax.all_gather(key_rows, "inner", axis=0, tiled=True),
        lax.all_gather(value_rows, "inner", axis=0, tiled=True),
        lax.all_gather(earlier_k, "inner", axis=0, tiled=True),
        lax.all_gather(earlier_v, "inner", axis=0, tiled=True),
    )
    padding = jnp.zeros((pad_blocks * block_len, width), key_rows.dtype)
    keys_all = jnp.concatenate([prior_k, group_k, padding], axis=0)
    values_all = jnp.concatenate([prior_v, group_v, padding], axis=0)
    first_block = inner_at * blocks_dev
    key_win = lax.dynamic_slice_in_dim(keys_all, first_block * block_len, win_blocks * block_len, 0)
    value_win = lax.dynamic_slice_in_dim(
        values_all, first_block * block_len, win_blocks * block_len, 0
    )
    tags_pad = jnp.concatenate(
        [
            jnp.full((span_blocks,), -1, jnp.int32),
            doc_blocks,
            jnp.full((span_blocks + pad_blocks,), -1, jnp.int32),
        ]
    )
    key_tags = lax.dynamic_slice_in_dim(
        tags_pad, outer_at * span_blocks + first_block, win_blocks, 0
    )
    own_tags = lax.dynamic_slice_in_dim(
        doc_blocks, (outer_at * inner_count + inner_at) * blocks_dev, blocks_dev, 0
    )
    row_tags = jnp.repeat(jnp.repeat(own_tags, block_len), head_count)
    row_pos = (
        jnp.repeat(jnp.arange(token_count, dtype=jnp.int32), head_count) + span_blocks * block_len
    )
    key_tiles = key_win.reshape(tile_count, tile_len, width)
    value_tiles = value_win.reshape(tile_count, tile_len, width)
    tag_tiles = jnp.repeat(key_tags, block_len).reshape(tile_count, tile_len)
    pos_tiles = jnp.arange(win_blocks * block_len, dtype=jnp.int32).reshape(tile_count, tile_len)
    query_flat = queries.reshape(token_count * head_count, width)
    grad_flat = grad_output.reshape(token_count * head_count, width)
    row_total = token_count * head_count

    def allowed_of(tag_tile, pos_tile):
        return (row_tags[:, None] == tag_tile[None, :]) & (pos_tile[None, :] <= row_pos[:, None])

    def forward_tile(running, pieces):
        key_tile, value_tile, tag_tile, pos_tile = pieces
        allowed = allowed_of(tag_tile, pos_tile)
        row_max, row_sum, out_acc = running
        scores = (
            jnp.einsum("rd,kd->rk", query_flat, key_tile, preferred_element_type=jnp.float32)
            * scaling
        )
        masked = jnp.where(allowed, scores, -jnp.inf)
        new_max = jnp.maximum(row_max, jnp.max(masked, axis=1, keepdims=True))
        factor = jnp.exp(row_max - new_max)
        weights = jnp.exp(masked - new_max)
        new_sum = row_sum * factor + jnp.sum(weights, axis=1, keepdims=True)
        weights_high = weights.astype(jnp.bfloat16)
        weights_rest = (weights - weights_high.astype(jnp.float32)).astype(jnp.bfloat16)
        product = jnp.dot(weights_high, value_tile, preferred_element_type=jnp.float32)
        product = product + jnp.dot(weights_rest, value_tile, preferred_element_type=jnp.float32)
        new_out = out_acc * factor + product
        return ((new_max, new_sum, new_out), None)

    start_state = (
        jnp.full((row_total, 1), -1e30, jnp.float32),
        jnp.zeros((row_total, 1), jnp.float32),
        jnp.zeros((row_total, width), jnp.float32),
    )
    (row_max, row_sum, out_acc), unused_ys = lax.scan(
        forward_tile, start_state, (key_tiles, value_tiles, tag_tiles, pos_tiles)
    )
    attn_out = out_acc / row_sum
    delta = jnp.sum(grad_flat.astype(jnp.float32) * attn_out, axis=1, keepdims=True)

    def backward_tile(grad_q, pieces):
        key_tile, value_tile, tag_tile, pos_tile = pieces
        allowed = allowed_of(tag_tile, pos_tile)
        scores = (
            jnp.einsum("rd,kd->rk", query_flat, key_tile, preferred_element_type=jnp.float32)
            * scaling
        )
        probs = jnp.exp(jnp.where(allowed, scores - row_max, -jnp.inf)) / row_sum
        probs_low = probs.astype(jnp.bfloat16)
        value_part = jnp.einsum(
            "rk,rd->kd", probs_low, grad_flat, preferred_element_type=jnp.float32
        )
        dprobs = jnp.einsum("rd,kd->rk", grad_flat, value_tile, preferred_element_type=jnp.float32)
        dscores = (probs * (dprobs - delta) * scaling).astype(jnp.bfloat16)
        new_q = grad_q + jnp.dot(dscores, key_tile, preferred_element_type=jnp.float32)
        key_part = jnp.einsum("rk,rd->kd", dscores, query_flat, preferred_element_type=jnp.float32)
        return (new_q, (key_part, value_part))

    grad_q, (key_parts, value_parts) = lax.scan(
        backward_tile,
        jnp.zeros((row_total, width), jnp.float32),
        (key_tiles, value_tiles, tag_tiles, pos_tiles),
    )
    grads_win = jnp.concatenate(
        [
            key_parts.reshape(win_blocks * block_len, width),
            value_parts.reshape(win_blocks * block_len, width),
        ],
        axis=1,
    )
    canvas = jnp.zeros(((2 * span_blocks + pad_blocks) * block_len, 2 * width), jnp.float32)
    canvas = lax.dynamic_update_slice_in_dim(canvas, grads_win, first_block * block_len, 0)
    earlier_part = canvas[: span_blocks * block_len]
    group_part = canvas[span_blocks * block_len : 2 * span_blocks * block_len]
    combined = jnp.concatenate([group_part, earlier_part], axis=1)
    summed = lax.psum_scatter(
        combined.astype(jnp.bfloat16), "inner", scatter_dimension=0, tiled=True
    ).astype(jnp.float32)
    returned = shifted(summed[:, 2 * width :].astype(jnp.bfloat16), "outer", -1).astype(jnp.float32)
    grads_kv = summed[:, : 2 * width] + returned
    grad_queries = grad_q.reshape(token_count, head_count * width).astype(jnp.bfloat16)
    return (
        grad_queries,
        grads_kv[:, :width].astype(jnp.bfloat16),
        grads_kv[:, width:].astype(jnp.bfloat16),
    )


def solution(mesh):
    in_specs = (
        P(("outer", "inner"), None),
        P(("outer", "inner"), None),
        P(("outer", "inner"), None),
        P(("outer", "inner"), None),
        P(),
    )
    out_specs = (
        P(("outer", "inner"), None),
        P(("outer", "inner"), None),
        P(("outer", "inner"), None),
    )
    return jax.shard_map(shards, mesh=mesh, in_specs=in_specs, out_specs=out_specs, check_vma=False)
```

profile of v0, /device:TPU:1, one launch (start us, length us, event | category | flops | bytes accessed | tf_op | source)
XLA Modules:
  0.0 564.5 jit_solution(11450851049235379509)
XLA Ops:
  8.7 3.9 collective-permute-start
  12.6 1.3 collective-permute-done
  14.7 3.5 collective-permute-start.1
  18.2 1.3 collective-permute-done.1
  20.3 1.3 dynamic_slice.40
  24.9 67.7 %all-gather.7.cloned.1.call-done = bf16[4096,128]{1,0:T(8,128)(2,1)} async-done(((bf16[128,128]{1,0:T(8,128)(2,1)}), bf16[4096,128]{1,0:T(8,128)(2,1)}) %all-gather.7.cloned.1.call-update) | async-done | bytes 1048592 | tf_op jit(solution)/shard_map/all_gather | solution.py:32
  92.6 77.2 %all-gather.11.cloned.1.call-done = bf16[4096,128]{1,0:T(8,128)(2,1)} async-done(((bf16[128,128]{1,0:T(8,128)(2,1)}), bf16[4096,128]{1,0:T(8,128)(2,1)}) %all-gather.11.cloned.1.call-update) | async-done | bytes 1048592 | tf_op jit(solution)/shard_map/all_gather | solution.py:33
  169.8 77.8 %all-gather.5.cloned.1.call-done = bf16[4096,128]{1,0:T(8,128)(2,1)} async-done(((bf16[128,128]{1,0:T(8,128)(2,1)}), bf16[4096,128]{1,0:T(8,128)(2,1)}) %all-gather.5.cloned.1.call-update) | async-done | bytes 1048592 | tf_op jit(solution)/shard_map/all_gather | solution.py:34
  247.5 77.6 %all-gather.9.cloned.1.call-done = bf16[4096,128]{1,0:T(8,128)(2,1)} async-done(((bf16[128,128]{1,0:T(8,128)(2,1)}), bf16[4096,128]{1,0:T(8,128)(2,1)}) %all-gather.9.cloned.1.call-update) | async-done | bytes 1048592 | tf_op jit(solution)/shard_map/all_gather | solution.py:35
  325.2 5.2 fusion.43
  330.4 35.2 %while.30 = (s32[]{:T(128)}, f32[1024,1]{0,1:T(1,128)S(1)}, f32[1024,1]{0,1:T(1,128)S(1)}, f32[1024,128]{1,0:T(8,128)S(1)}, s32[9,512]{1,0:T(8,128)S(1)}, /*inde...) while((s32[]{:T(128)}, f32[1024,1]{0,1:T(1,128)S(1)}, ...), condition=%wide.region_3.4_spmd.clone, body=%wide.region_0.3_spmd.clone.sunk | while | flops 410524160 | bytes 11240605 | solution.py:98
  331.2 1.5 fusion.84
  335.1 1.5 fusion.84
  339.0 1.6 fusion.84
  342.9 1.5 fusion.84
  346.9 1.5 fusion.84
  350.8 1.6 fusion.84
  354.7 1.5 fusion.84
  358.6 1.5 fusion.84
  362.5 1.6 fusion.84
  366.0 60.3 %while.31 = (s32[]{:T(128)}, f32[1024,128]{1,0:T(8,128)S(1)}, bf16[9,512,128]{2,1,0:T(8,128)(2,1)}, bf16[9,512,128]{2,1,0:T(8,128)(2,1)}, s32[9,512]{1,0:T(8,128...) while((s32[]{:T(128)}, f32[1024,128]{1,0:T(8,128)S(1)}, ...), condition=%wide.region_6.7_spmd.clone, body=%wide.region_5.6_spmd.clone.sunk | while | flops 677119488 | bytes 12494019 | solution.py:122
  366.8 1.8 fusion.100
  370.1 1.5 convolution_add_fusion.3
  373.5 1.7 fusion.100
  376.8 1.5 convolution_add_fusion.3
  380.2 1.7 fusion.100
  382.4 1.1 fusion.103
  383.5 1.5 convolution_add_fusion.3
  385.0 1.1 fusion.102
  386.9 1.7 fusion.100
  389.1 1.1 fusion.103
  390.2 1.5 convolution_add_fusion.3
  393.6 1.7 fusion.100
  396.9 1.5 convolution_add_fusion.3
  400.3 1.8 fusion.100
  403.6 1.5 convolution_add_fusion.3
  407.0 1.7 fusion.100
  409.2 1.1 fusion.103
  410.3 1.5 convolution_add_fusion.3
  413.7 1.8 fusion.100
  417.0 1.5 convolution_add_fusion.3
  420.4 1.7 fusion.100
  422.6 1.1 fusion.103
  423.7 1.5 convolution_add_fusion.3
  428.7 2.3 pad_maximum_fusion
  431.1 119.6 %reduce-scatter.2.cloned.1.call-done = bf16[128,512]{1,0:T(8,128)(2,1)} async-done(((bf16[4096,512]{1,0:T(8,128)(2,1)}), bf16[128,512]{1,0:T(8,128)(2,1)}) %reduce-scatter.2.cloned.1.call-update) | async-done | bytes 131088 | tf_op jit(solution)/shard_map/reduce_scatter | solution.py:139
  551.5 1.3 collective-permute-start.2
  553.6 2.9 collective-permute-done.2
  (194 shorter events, 57.9 us)
Async XLA Ops:
  7.2 85.4 %all-gather.7.cloned.1.call-start = ((), (), s32[]{:S(2)}) async-start(), calls=%async_computation.2 | async-start | bytes 1081344 | tf_op jit(solution)/shard_map/all_gather | solution.py:32
  7.9 161.9 %all-gather.11.cloned.1.call-start = ((), (), s32[]{:S(2)}) async-start(), calls=%async_computation.4 | async-start | bytes 1081344 | tf_op jit(solution)/shard_map/all_gather | solution.py:33
  8.6 238.9 %all-gather.5.cloned.1.call-start = ((), (), s32[]{:S(2)}) async-start(), calls=%async_computation.1 | async-start | bytes 1081344 | tf_op jit(solution)/shard_map/all_gather | solution.py:34
  8.7 5.3 collective-permute-start
  14.0 0.6 copy-start.2
  14.6 310.6 %all-gather.9.cloned.1.call-start = ((), (), s32[]{:S(2)}) async-start(), calls=%async_computation.3 | async-start | bytes 1081344 | tf_op jit(solution)/shard_map/all_gather | solution.py:35
  14.7 4.9 collective-permute-start.1
  19.5 0.6 copy-start.3
  20.2 530.5 %reduce-scatter.2.cloned.1.call-start = ((), (), s32[]{:S(2)}) async-start(), calls=%async_computation.5 | async-start | bytes 4325376 | tf_op jit(solution)/shard_map/reduce_scatter | solution.py:139
  426.3 1.3 copy-start
  426.3 1.6 copy-start.1
  551.5 5.0 collective-permute-start.2
Sparse Core Ops, SparseCore 0:
  10.8 81.7 all-gather.6
  95.4 74.3 all-gather.10
  173.1 74.3 all-gather.4
  250.8 74.3 all-gather.8
  431.2 119.4 reduce-scatter.1
where the time goes:
time: 573 us; the launch traced here: 564 us
  waiting for transfers between devices  427 us (75%)
  matrix products  77.1 us (13%)
  other arithmetic  25.6 us (4%)
  between operations  13.9 us (2%)
  local copies, waits for them, and re-layouts  11 us (2%)
  starting transfers between devices  8.96 us (2%)
    reduce_scatter x1, waiting for transfers between devices, shards(): lax.psum_scatter(combined.astype(jnp.bfloat16), 'inner', scatter_dimensio...  120 us
    all_gather x1, waiting for transfers between devices, shards(): lax.all_gather(earlier_k, 'inner', axis=0, tiled=True)  77.8 us
    all_gather x1, waiting for transfers between devices, shards(): lax.all_gather(earlier_v, 'inner', axis=0, tiled=True)  77.6 us
    all_gather x1, waiting for transfers between devices, shards(): lax.all_gather(value_rows, 'inner', axis=0, tiled=True)  77.2 us
    all_gather x1, waiting for transfers between devices, shards(): lax.all_gather(key_rows, 'inner', axis=0, tiled=True)  67.7 us
    dot_general x9, matrix products, backward_tile(): jnp.einsum('rd,kd->rk', query_flat, key_tile, preferred_element_type=jnp....  15.7 us
    dot_general x9, matrix products, forward_tile(): jnp.einsum('rd,kd->rk', query_flat, key_tile, preferred_element_type=jnp....  13.9 us
    dot_general x9, matrix products, backward_tile(): jnp.dot(dscores, key_tile, preferred_element_type=jnp.float32)  13.5 us
  transfers between devices with their start and end apart: 8, of which 8 were waited for; matrix products, arithmetic and copies ran while one was open for 1% of the time, Pallas kernels for 0%

commit v1 on v0

v1 whole, which is shorter than its diff:
```python
import functools
import math

import jax
import jax.numpy as jnp
from jax import lax
from jax.experimental import pallas as pl
from jax.experimental.pallas import tpu as pltpu
from jax.sharding import PartitionSpec as P

MESH = pl.DeviceIdType.MESH
WINDOW = 16
LINE = WINDOW // 2
SLOTS = WINDOW + 1
COLS = 256
LOW = -1e30
HIGH = 3e38


def nearest(n):
    n = n + 1
    half = n // 2
    k = half + (n % 2) * (LINE - 2 * half)
    return jnp.where(k == 0, LINE, k)


def farthest(n):
    return nearest(LINE - 1 - n)


def kernel(
    inner_count,
    chips,
    blk,
    width,
    heads,
    q_ref,
    k_ref,
    v_ref,
    do_ref,
    doc_ref,
    dq_ref,
    dk_ref,
    dv_ref,
    kv,
    keys_t,
    rows_q,
    rows_do,
    cols_q,
    cols_do,
    weights,
    dprobs,
    tile_max,
    run_max,
    run_sum,
    run_dot,
    own_stats,
    other_stats,
    low,
    dsc,
    out_buf,
    from_pair,
    from_line,
    own_part,
    dq_send,
    dq_recv,
    line_send,
    line_recv,
    pair_send,
    pair_recv,
    back_pair_send,
    back_pair_recv,
    back_line_send,
    back_line_recv,
    core_send,
    core_recv,
):
    rows = heads * blk
    tiles = rows // COLS
    both = 2 * tiles
    scale = width ** (-0.5)
    scale2 = scale * math.log2(math.e)
    per_group = inner_count // 2

    outer = lax.axis_index("outer")
    inner = lax.axis_index("inner")
    core = inner % 2
    chip = outer * per_group + inner // 2
    odd = chip % 2

    def device(chip_at, core_at):
        return {
            "outer": chip_at // per_group,
            "inner": (chip_at % per_group) * 2 + core_at,
        }

    def later(k):
        return device((chip + 2 * k) % chips, core)

    def earlier(k):
        return device((chip - 2 * k + chips) % chips, core)

    other_core = device(chip, 1 - core)
    pair = device(chip + 1 - 2 * odd, core)

    def copy(src, dst, send, recv, to):
        return pltpu.make_async_remote_copy(
            src_ref=src,
            dst_ref=dst,
            send_sem=send,
            recv_sem=recv,
            device_id=to,
            device_id_type=MESH,
        )

    def line_copy(k):
        return copy(
            kv.at[0], kv.at[2 * k], line_send.at[k], line_recv.at[k], later(k)
        )

    def pair_copy(m):
        b = m + 1 - odd
        return copy(
            kv.at[2 * m], kv.at[2 * b - 1], pair_send.at[b], pair_recv.at[b], pair
        )

    def pair_arrival(b):
        return copy(
            kv.at[0], kv.at[2 * b - 1], pair_send.at[b], pair_recv.at[b], pair
        )

    def back_pair_copy(b):
        m = b - odd
        return copy(
            out_buf.at[2 * b - 1],
            from_pair.at[m],
            back_pair_send.at[m],
            back_pair_recv.at[m],
            pair,
        )

    def back_pair_arrival(m):
        return copy(
            out_buf.at[0],
            from_pair.at[m],
            back_pair_send.at[m],
            back_pair_recv.at[m],
            pair,
        )

    def back_line_copy(k):
        return copy(
            out_buf.at[2 * k],
            from_line.at[k],
            back_line_send.at[k],
            back_line_recv.at[k],
            earlier(k),
        )

    def core_copies():
        own = pl.ds(pl.multiple_of(core * rows, rows), rows)
        return (
            copy(
                rows_q.at[own], rows_q.at[own], core_send.at[0], core_recv.at[0],
                other_core,
            ),
            copy(
                rows_do.at[own], rows_do.at[own], core_send.at[1], core_recv.at[1],
                other_core,
            ),
        )

    def core_arrivals():
        own = pl.ds(pl.multiple_of((1 - core) * rows, rows), rows)
        return (
            copy(
                rows_q.at[own], rows_q.at[own], core_send.at[0], core_recv.at[0],
                other_core,
            ),
            copy(
                rows_do.at[own], rows_do.at[own], core_send.at[1], core_recv.at[1],
                other_core,
            ),
        )

    barrier = pltpu.get_barrier_semaphore()
    for k in range(1, LINE + 1):
        for to in (later(k), earlier(k)):
            pl.semaphore_signal(barrier, inc=1, device_id=to, device_id_type=MESH)
    for to in (other_core, pair):
        pl.semaphore_signal(barrier, inc=1, device_id=to, device_id_type=MESH)

    kv[0, :, :width] = k_ref[...]
    kv[0, :, width:] = v_ref[...]
    for h in range(heads):
        at = pl.ds(pl.multiple_of(core * rows + h * blk, blk), blk)
        rows_q[at, :] = q_ref[:, h * width : (h + 1) * width]
        rows_do[at, :] = do_ref[:, h * width : (h + 1) * width]
    run_max[...] = jnp.full(run_max.shape, LOW, jnp.float32)
    run_sum[...] = jnp.zeros(run_sum.shape, jnp.float32)
    run_dot[...] = jnp.zeros(run_dot.shape, jnp.float32)

    pl.semaphore_wait(barrier, 2 * LINE + 2)

    def start_line(n, carry):
        line_copy(nearest(n)).start()
        return carry

    for c in core_copies():
        c.start()
    lax.fori_loop(0, LINE, start_line, 0)

    @pl.when(odd == 0)
    def _():
        pair_copy(0).start()

    def columns(base):
        def one(i, carry):
            at = pl.ds(pl.multiple_of(base + i * blk, blk), blk)
            cols_q[:, at] = rows_q[at, :].T
            cols_do[:, at] = rows_do[at, :].T
            return carry

        lax.fori_loop(0, heads, one, 0)

    columns(core * rows)
    for c in core_arrivals():
        c.wait_recv()
    columns((1 - core) * rows)

    def forward(slot, own):
        key_chip = (chip - slot + chips) % chips
        key_block = 2 * key_chip + core
        key_tag = doc_ref[key_block]
        key_tile = kv[slot, :, :width]
        value_tile = kv[slot, :, width:]
        keys_t[:, pl.ds(pl.multiple_of(slot * blk, blk), blk)] = key_tile.T

        def tile(i, carry):
            at = pl.ds(pl.multiple_of(i * COLS, COLS), COLS)
            query_half = i // tiles
            query_block = 2 * chip + query_half
            seen = (key_tag == doc_ref[query_block]) & (key_block <= query_block)
            s = jnp.dot(key_tile, cols_q[:, at], preferred_element_type=jnp.float32)
            dp = jnp.dot(value_tile, cols_do[:, at], preferred_element_type=jnp.float32)
            s = s * scale2
            if own:
                key_at = lax.broadcasted_iota(jnp.int32, (blk, COLS), 0)
                query_at = lax.broadcasted_iota(jnp.int32, (blk, COLS), 1) % blk
                s = jnp.where(
                    key_at - query_at <= (query_half - core) * blk, s, 2 * LOW
                )
            s3 = s.reshape(blk // 8, 8, COLS)
            dp3 = dp.reshape(blk // 8, 8, COLS)
            top = jnp.max(s3, axis=0)
            old = run_max[:, at]
            new = jnp.where(seen, jnp.maximum(old, top), old)
            used = jnp.where(seen, new, HIGH)
            w = jnp.exp2(s3 - used[None])
            factor = jnp.exp2(old - new)
            run_max[:, at] = new
            tile_max[slot, :, at] = new
            run_sum[:, at] = run_sum[:, at] * factor + jnp.sum(w, axis=0)
            run_dot[:, at] = run_dot[:, at] * factor + jnp.sum(w * dp3, axis=0)
            weights[slot, :, at] = w.reshape(blk, COLS)
            dprobs[slot, :, at] = dp
            return carry

        lax.fori_loop(0, both, tile, 0)

    forward(0, True)

    def gather_step(n, carry):
        @pl.when(n < LINE)
        def _():
            k = nearest(n)
            line_copy(k).wait_recv()

            @pl.when((k < LINE) | (odd == 1))
            def _():
                pair_copy(k).start()

            forward(2 * k, False)

        @pl.when(n > 0)
        def _():
            k = nearest(n - 1)
            b = jnp.where(odd == 1, k % LINE + 1, k)
            pair_arrival(b).wait_recv()
            forward(2 * b - 1, False)

        return carry

    lax.fori_loop(0, LINE + 1, gather_step, 0)

    m8 = run_max[...]
    m1 = jnp.max(m8, axis=0, keepdims=True)
    f8 = jnp.exp2(m8 - m1)
    own_stats[0:1, :] = m1
    own_stats[1:2, :] = jnp.sum(run_sum[...] * f8, axis=0, keepdims=True)
    own_stats[2:3, :] = jnp.sum(run_dot[...] * f8, axis=0, keepdims=True)
    stats_copy = copy(
        own_stats, other_stats, core_send.at[2], core_recv.at[2], other_core
    )
    stats_copy.start()
    stats_copy.wait()
    ma, mb = own_stats[0:1, :], other_stats[0:1, :]
    m1 = jnp.maximum(ma, mb)
    fa, fb = jnp.exp2(ma - m1), jnp.exp2(mb - m1)
    total = own_stats[1:2, :] * fa + other_stats[1:2, :] * fb
    delta = (own_stats[2:3, :] * fa + other_stats[2:3, :] * fb) / total
    run_max[...] = jnp.broadcast_to(m1, run_max.shape)
    run_sum[...] = jnp.broadcast_to(1.0 / total, run_sum.shape)
    run_dot[...] = jnp.broadcast_to(delta, run_dot.shape)

    def backward(slot):
        def tile(i, carry):
            at = pl.ds(pl.multiple_of(i * COLS, COLS), COLS)
            factor = jnp.exp2(tile_max[slot, :, at] - run_max[:, at]) * run_sum[:, at]
            p3 = weights[slot, :, at].reshape(blk // 8, 8, COLS) * factor[None]
            dp3 = dprobs[slot, :, at].reshape(blk // 8, 8, COLS)
            ds3 = p3 * (dp3 - run_dot[:, at][None])
            low[:, at] = p3.reshape(blk, COLS).astype(jnp.bfloat16)
            dsc[pl.ds(pl.multiple_of(slot * blk, blk), blk), at] = ds3.reshape(
                blk, COLS
            ).astype(jnp.bfloat16)
            return carry

        lax.fori_loop(0, both, tile, 0)
        dv = jnp.dot(low[...], rows_do[...], preferred_element_type=jnp.float32)
        dk = jnp.dot(
            dsc[pl.ds(pl.multiple_of(slot * blk, blk), blk), :],
            rows_q[...],
            preferred_element_type=jnp.float32,
        )
        return dk * scale, dv

    @pl.when(odd == 0)
    def _():
        from_pair[LINE] = jnp.zeros(from_pair.shape[1:], jnp.bfloat16)

    @pl.when(odd == 1)
    def _():
        from_pair[0] = jnp.zeros(from_pair.shape[1:], jnp.bfloat16)

    def return_step(n, carry):
        @pl.when(n < LINE)
        def _():
            k = farthest(n)
            b = jnp.where(odd == 1, k % LINE + 1, k)
            dk, dv = backward(2 * b - 1)
            out_buf[2 * b - 1, :, :width] = dk.astype(jnp.bfloat16)
            out_buf[2 * b - 1, :, width:] = dv.astype(jnp.bfloat16)
            back_pair_copy(b).start()

        @pl.when(n > 0)
        def _():
            k = farthest(n - 1)
            dk, dv = backward(2 * k)

            @pl.when((k < LINE) | (odd == 1))
            def _():
                back_pair_arrival(k).wait_recv()

            got = from_pair[k].astype(jnp.float32)
            out_buf[2 * k, :, :width] = (dk + got[:, :width]).astype(jnp.bfloat16)
            out_buf[2 * k, :, width:] = (dv + got[:, width:]).astype(jnp.bfloat16)
            back_line_copy(k).start()

        return carry

    lax.fori_loop(0, LINE + 1, return_step, 0)

    dk, dv = backward(0)
    own_part[:, :width] = dk
    own_part[:, width:] = dv

    def query_tile(i):
        at = pl.ds(pl.multiple_of(i * blk, blk), blk)
        part = jnp.dot(keys_t[...], dsc[:, at], preferred_element_type=jnp.float32)
        return (part * scale).T

    def far_rows(i, carry):
        at = pl.ds(pl.multiple_of(i * width, width), width)
        dq_send[:, at] = query_tile((1 - core) * heads + i).astype(jnp.bfloat16)
        return carry

    lax.fori_loop(0, heads, far_rows, 0)
    dq_copy = copy(dq_send, dq_recv, core_send.at[3], core_recv.at[3], other_core)
    dq_copy.start()

    def near_rows(i, carry):
        at = pl.ds(pl.multiple_of(i * width, width), width)
        near = query_tile(core * heads + i)
        dq_ref[:, at] = (near + dq_recv[:, at].astype(jnp.float32)).astype(jnp.bfloat16)
        return carry

    dq_copy.wait()
    lax.fori_loop(0, heads, near_rows, 0)

    @pl.when(odd == 0)
    def _():
        back_pair_arrival(0).wait_recv()

    own_part[...] += from_pair[0].astype(jnp.float32)

    def add_line(n, carry):
        k = farthest(n)
        back_line_copy(k).wait_recv()
        own_part[...] += from_line[k].astype(jnp.float32)
        return carry

    lax.fori_loop(0, LINE, add_line, 0)
    dk_ref[...] = own_part[:, :width].astype(jnp.bfloat16)
    dv_ref[...] = own_part[:, width:].astype(jnp.bfloat16)

    def finish(n, carry):
        k = n + 1
        line_copy(k).wait_send()
        back_line_copy(k).wait_send()
        pair_copy(n + odd).wait_send()
        back_pair_copy(k).wait_send()
        return carry

    lax.fori_loop(0, LINE, finish, 0)
    for c in core_copies():
        c.wait_send()


def solution(mesh):
    inner_count = mesh.shape["inner"]
    devices = inner_count * mesh.shape["outer"]

    def shards(queries, key_rows, value_rows, grad_output, doc_blocks):
        blk, width = key_rows.shape
        heads = queries.shape[1] // width
        rows = heads * blk
        bf16, f32 = jnp.bfloat16, jnp.float32
        vmem = pl.BlockSpec(memory_space=pltpu.VMEM)
        dma = pltpu.SemaphoreType.DMA
        return pl.pallas_call(
            functools.partial(kernel, inner_count, devices // 2, blk, width, heads),
            name="attention_backward",
            out_shape=(
                jax.ShapeDtypeStruct(queries.shape, bf16),
                jax.ShapeDtypeStruct(key_rows.shape, bf16),
                jax.ShapeDtypeStruct(value_rows.shape, bf16),
            ),
            in_specs=[vmem] * 4 + [pl.BlockSpec(memory_space=pltpu.SMEM)],
            out_specs=(vmem, vmem, vmem),
            scratch_shapes=[
                pltpu.VMEM((SLOTS, blk, 2 * width), bf16),
                pltpu.VMEM((width, SLOTS * blk), bf16),
                pltpu.VMEM((2 * rows, width), bf16),
                pltpu.VMEM((2 * rows, width), bf16),
                pltpu.VMEM((width, 2 * rows), bf16),
                pltpu.VMEM((width, 2 * rows), bf16),
                pltpu.VMEM((SLOTS, blk, 2 * rows), f32),
                pltpu.VMEM((SLOTS, blk, 2 * rows), f32),
                pltpu.VMEM((SLOTS, 8, 2 * rows), f32),
                pltpu.VMEM((8, 2 * rows), f32),
                pltpu.VMEM((8, 2 * rows), f32),
                pltpu.VMEM((8, 2 * rows), f32),
                pltpu.VMEM((3, 2 * rows), f32),
                pltpu.VMEM((3, 2 * rows), f32),
                pltpu.VMEM((blk, 2 * rows), bf16),
                pltpu.VMEM((SLOTS * blk, 2 * rows), bf16),
                pltpu.VMEM((SLOTS, blk, 2 * width), bf16),
                pltpu.VMEM((LINE + 1, blk, 2 * width), bf16),
                pltpu.VMEM((LINE + 1, blk, 2 * width), bf16),
                pltpu.VMEM((blk, 2 * width), f32),
                pltpu.VMEM((blk, heads * width), bf16),
                pltpu.VMEM((blk, heads * width), bf16),
                dma((LINE + 1,)),
                dma((LINE + 1,)),
                dma((LINE + 1,)),
                dma((LINE + 1,)),
                dma((LINE + 1,)),
                dma((LINE + 1,)),
                dma((LINE + 1,)),
                dma((LINE + 1,)),
                dma((4,)),
                dma((4,)),
            ],
            compiler_params=pltpu.CompilerParams(
                collective_id=0, has_side_effects=True, vmem_limit_bytes=60 << 20
            ),
        )(queries, key_rows, value_rows, grad_output, doc_blocks)

    rows = P(("outer", "inner"), None)
    return jax.shard_map(
        shards,
        mesh=mesh,
        in_specs=(rows, rows, rows, rows, P()),
        out_specs=(rows, rows, rows),
        check_vma=False,
    )
```

time: 573 us -> 94.5 us (0.16); the launches traced: 564 us -> 94.3 us
  waiting for transfers between devices: 427 us -> 0 us
  Pallas kernels: 0 us -> 90.6 us
  matrix products: 77.1 us -> 0 us
  other arithmetic: 25.6 us -> 0 us
  between operations: 13.9 us -> 0.65 us
  starting transfers between devices: 8.96 us -> 0 us
  local copies, waits for them, and re-layouts: 11 us -> 3.06 us
    all_gather x4 -> x0, waiting for transfers between devices: 300 us -> none  [the longest x1 77.8 us: shards(): lax.all_gather(earlier_k, 'inner', axis=0, tiled=True)]
    reduce_scatter x1 -> x0, waiting for transfers between devices: 120 us -> none  [shards(): lax.psum_scatter(combined.astype(jnp.bfloat16), 'inner', scatter_dimensio...]
    pallas_call x0 -> x1, Pallas kernels: none -> 90.6 us  [shards(): pl.pallas_call(functools.partial(kernel, inner_count, devices // 2, blk,...]
    dot_general x72 -> x0, matrix products: 77.1 us -> none  [the longest x9 15.7 us: backward_tile(): jnp.einsum('rd,kd->rk', query_flat, key_tile, preferred_element_type=jnp....]
    eq x18 -> x0, other arithmetic: 12.1 us -> none  [allowed_of(): row_tags[:, None] == tag_tile[None, :]]
    ppermute x3 -> x0, starting transfers between devices: 8.77 us -> none  [shifted(): return lax.ppermute(block, axis, route)]
    concatenate x3 -> x0, other arithmetic: 8.26 us -> none  [the longest x1 5.22 us: shards(): values_all = jnp.concatenate([prior_v, group_v, padding], axis=0)]
  transfers between devices with their start and end apart: 8 -> 0, of which waited for: 8 -> 0; matrix products, arithmetic and copies ran while one was open for 1% -> 0% of each run, Pallas kernels for 0% -> 0%
where the time goes in v1:
time: 94.5 us; the launch traced here: 94.3 us
  Pallas kernels  90.6 us (96%)
  local copies, waits for them, and re-layouts  3.06 us (3%)
    pallas_call x1, Pallas kernels, shards(): pl.pallas_call(functools.partial(kernel, inner_count, devices // 2, blk,...  90.6 us
    unnamed x7, local copies, waits for them, and re-layouts  3.06 us

profile of v1, /device:TPU:1, one launch (start us, length us, event | category | flops | bytes accessed | tf_op | source)
XLA Modules:
  0.0 94.3 jit_solution(957130944022733383)
XLA Ops:
  0.6 90.6 %attention_backward.1 = (bf16[128,1024]{1,0:T(8,128)(2,1)}, bf16[128,128]{1,0:T(8,128)(2,1)}, bf16[128,128]{1,0:T(8,128)(2,1)}) custom-call(bf16[128,1024]{1,0:T(8,128)(2,1)} %q_ref.1, bf16[128,128]{1,0:T(8,128)(2,1)} %k_ref.1, bf16[128,128]{1,0:T(8,128)(2,1)} %v_ref.1, bf16[128,1024]{1,0:T(8,128)(2,1)} %do_ref.1, s32[256]{0:T(256)} %doc_ref.1), custom_call_target="tpu_custom_call" | custom-call | tf_op jit(solution)/shard_map/attention_backward/pallas_call | solution.py:441
  91.2 0.0 copy-start.1
  91.3 1.7 %copy.11 = bf16[128,1024]{1,0:T(8,128)(2,1)} copy(bf16[128,1024]{1,0:T(8,128)(2,1)} %get-tuple-element.6) | data formatting | bytes 524288
  92.9 0.0 copy-done.1
  92.9 0.0 copy-start
  92.9 0.6 copy.12
  93.5 0.2 copy-done
  93.7 0.6 copy.13
Async XLA Ops:
  91.2 1.7 %copy-start.1 = (bf16[128,128]{1,0:T(8,128)(2,1)S(1)}, bf16[128,128]{1,0:T(8,128)(2,1)}, u32[]{:S(2)}) copy-start(bf16[128,128]{1,0:T(8,128)(2,1)} %get-tuple-element.7) | copy-start | bytes 98308
  92.9 0.8 copy-start

commit v2 on v1

--- a/solution.py
+++ b/solution.py
@@ -13,6 +13,9 @@
 LINE = WINDOW // 2
 SLOTS = WINDOW + 1
 COLS = 256
+AHEAD = 8
+LAG = 3
+BACK_LAG = 3
 LOW = -1e30
 HIGH = 3e38
 
@@ -62,6 +65,7 @@
     from_pair,
     from_line,
     own_part,
+    near,
     dq_send,
     dq_recv,
     line_send,
@@ -208,7 +212,7 @@
 
     for c in core_copies():
         c.start()
-    lax.fori_loop(0, LINE, start_line, 0)
+    lax.fori_loop(0, AHEAD, start_line, 0)
 
     @pl.when(odd == 0)
     def _():
@@ -236,8 +240,8 @@
         value_tile = kv[slot, :, width:]
         keys_t[:, pl.ds(pl.multiple_of(slot * blk, blk), blk)] = key_tile.T
 
-        def tile(i, carry):
-            at = pl.ds(pl.multiple_of(i * COLS, COLS), COLS)
+        def tile(i):
+            at = pl.ds(i * COLS, COLS)
             query_half = i // tiles
             query_block = 2 * chip + query_half
             seen = (key_tag == doc_ref[query_block]) & (key_block <= query_block)
@@ -264,9 +268,9 @@
             run_dot[:, at] = run_dot[:, at] * factor + jnp.sum(w * dp3, axis=0)
             weights[slot, :, at] = w.reshape(blk, COLS)
             dprobs[slot, :, at] = dp
-            return carry
-
-        lax.fori_loop(0, both, tile, 0)
+
+        for i in range(both):
+            tile(i)
 
     forward(0, True)
 
@@ -276,22 +280,26 @@
             k = nearest(n)
             line_copy(k).wait_recv()
 
+            @pl.when(n + AHEAD < LINE)
+            def _():
+                line_copy(nearest(n + AHEAD)).start()
+
             @pl.when((k < LINE) | (odd == 1))
             def _():
                 pair_copy(k).start()
 
             forward(2 * k, False)
 
-        @pl.when(n > 0)
+        @pl.when(n >= LAG)
         def _():
-            k = nearest(n - 1)
+            k = nearest(n - LAG)
             b = jnp.where(odd == 1, k % LINE + 1, k)
             pair_arrival(b).wait_recv()
             forward(2 * b - 1, False)
 
         return carry
 
-    lax.fori_loop(0, LINE + 1, gather_step, 0)
+    lax.fori_loop(0, LINE + LAG, gather_step, 0)
 
     m8 = run_max[...]
     m1 = jnp.max(m8, axis=0, keepdims=True)
@@ -314,8 +322,8 @@
     run_dot[...] = jnp.broadcast_to(delta, run_dot.shape)
 
     def backward(slot):
-        def tile(i, carry):
-            at = pl.ds(pl.multiple_of(i * COLS, COLS), COLS)
+        def tile(i):
+            at = pl.ds(i * COLS, COLS)
             factor = jnp.exp2(tile_max[slot, :, at] - run_max[:, at]) * run_sum[:, at]
             p3 = weights[slot, :, at].reshape(blk // 8, 8, COLS) * factor[None]
             dp3 = dprobs[slot, :, at].reshape(blk // 8, 8, COLS)
@@ -324,9 +332,9 @@
             dsc[pl.ds(pl.multiple_of(slot * blk, blk), blk), at] = ds3.reshape(
                 blk, COLS
             ).astype(jnp.bfloat16)
-            return carry
-
-        lax.fori_loop(0, both, tile, 0)
+
+        for i in range(both):
+            tile(i)
         dv = jnp.dot(low[...], rows_do[...], preferred_element_type=jnp.float32)
         dk = jnp.dot(
             dsc[pl.ds(pl.multiple_of(slot * blk, blk), blk), :],
@@ -353,9 +361,9 @@
             out_buf[2 * b - 1, :, width:] = dv.astype(jnp.bfloat16)
             back_pair_copy(b).start()
 
-        @pl.when(n > 0)
+        @pl.when(n >= BACK_LAG)
         def _():
-            k = farthest(n - 1)
+            k = farthest(n - BACK_LAG)
             dk, dv = backward(2 * k)
 
             @pl.when((k < LINE) | (odd == 1))
@@ -369,34 +377,40 @@
 
         return carry
 
-    lax.fori_loop(0, LINE + 1, return_step, 0)
+    lax.fori_loop(0, LINE + BACK_LAG, return_step, 0)
 
     dk, dv = backward(0)
     own_part[:, :width] = dk
     own_part[:, width:] = dv
 
     def query_tile(i):
-        at = pl.ds(pl.multiple_of(i * blk, blk), blk)
+        at = pl.ds(pl.multiple_of(i * COLS, COLS), COLS)
         part = jnp.dot(keys_t[...], dsc[:, at], preferred_element_type=jnp.float32)
         return (part * scale).T
 
+    heads_tile = COLS // blk
+
     def far_rows(i, carry):
-        at = pl.ds(pl.multiple_of(i * width, width), width)
-        dq_send[:, at] = query_tile((1 - core) * heads + i).astype(jnp.bfloat16)
-        return carry
-
-    lax.fori_loop(0, heads, far_rows, 0)
+        part = query_tile((1 - core) * tiles + i).astype(jnp.bfloat16)
+        for j in range(heads_tile):
+            at = pl.ds(pl.multiple_of((i * heads_tile + j) * width, width), width)
+            dq_send[:, at] = part[j * blk : (j + 1) * blk]
+        return carry
+
+    lax.fori_loop(0, tiles, far_rows, 0)
     dq_copy = copy(dq_send, dq_recv, core_send.at[3], core_recv.at[3], other_core)
     dq_copy.start()
 
     def near_rows(i, carry):
-        at = pl.ds(pl.multiple_of(i * width, width), width)
-        near = query_tile(core * heads + i)
-        dq_ref[:, at] = (near + dq_recv[:, at].astype(jnp.float32)).astype(jnp.bfloat16)
-        return carry
-
+        part = query_tile(core * tiles + i)
+        for j in range(heads_tile):
+            at = pl.ds(pl.multiple_of((i * heads_tile + j) * width, width), width)
+            near[:, at] = part[j * blk : (j + 1) * blk]
+        return carry
+
+    lax.fori_loop(0, tiles, near_rows, 0)
     dq_copy.wait()
-    lax.fori_loop(0, heads, near_rows, 0)
+    dq_ref[...] = (near[...] + dq_recv[...].astype(jnp.float32)).astype(jnp.bfloat16)
 
     @pl.when(odd == 0)
     def _():
@@ -469,6 +483,7 @@
                 pltpu.VMEM((LINE + 1, blk, 2 * width), bf16),
                 pltpu.VMEM((LINE + 1, blk, 2 * width), bf16),
                 pltpu.VMEM((blk, 2 * width), f32),
+                pltpu.VMEM((blk, heads * width), f32),
                 pltpu.VMEM((blk, heads * width), bf16),
                 pltpu.VMEM((blk, heads * width), bf16),
                 dma((LINE + 1,)),

time: 94.5 us -> 65.5 us (0.69)
  Pallas kernels: 90.6 us -> 61.6 us
    pallas_call x1, Pallas kernels: 90.6 us -> 61.6 us  [shards(): pl.pallas_call(functools.partial(kernel, inner_count, devices // 2, blk,...]
where the time goes in v2:
time: 65.5 us; the launch traced here: 65.3 us
  Pallas kernels  61.6 us (94%)
  local copies, waits for them, and re-layouts  3.06 us (5%)
    pallas_call x1, Pallas kernels, shards(): pl.pallas_call(functools.partial(kernel, inner_count, devices // 2, blk,...  61.6 us
    unnamed x7, local copies, waits for them, and re-layouts  3.06 us

profile of v2, /device:TPU:1, one launch (start us, length us, event | category | flops | bytes accessed | tf_op | source)
XLA Modules:
  0.0 65.3 jit_solution(2031740206342681806)
XLA Ops:
  0.6 61.6 %attention_backward.1 = (bf16[128,1024]{1,0:T(8,128)(2,1)}, bf16[128,128]{1,0:T(8,128)(2,1)}, bf16[128,128]{1,0:T(8,128)(2,1)}) custom-call(bf16[128,1024]{1,0:T(8,128)(2,1)} %q_ref.1, bf16[128,128]{1,0:T(8,128)(2,1)} %k_ref.1, bf16[128,128]{1,0:T(8,128)(2,1)} %v_ref.1, bf16[128,1024]{1,0:T(8,128)(2,1)} %do_ref.1, s32[256]{0:T(256)} %doc_ref.1), custom_call_target="tpu_custom_call" | custom-call | tf_op jit(solution)/shard_map/attention_backward/pallas_call | solution.py:455
  62.2 0.0 copy-start.1
  62.2 1.7 %copy.11 = bf16[128,1024]{1,0:T(8,128)(2,1)} copy(bf16[128,1024]{1,0:T(8,128)(2,1)} %get-tuple-element.6) | data formatting | bytes 524288
  63.9 0.0 copy-done.1
  63.9 0.0 copy-start
  63.9 0.6 copy.12
  64.5 0.2 copy-done
  64.7 0.6 copy.13
Async XLA Ops:
  62.2 1.7 %copy-start.1 = (bf16[128,128]{1,0:T(8,128)(2,1)S(1)}, bf16[128,128]{1,0:T(8,128)(2,1)}, u32[]{:S(2)}) copy-start(bf16[128,128]{1,0:T(8,128)(2,1)} %get-tuple-element.7) | copy-start | bytes 98308
  63.9 0.8 %copy-start = (bf16[128,128]{1,0:T(8,128)(2,1)S(1)}, bf16[128,128]{1,0:T(8,128)(2,1)}, u32[]{:S(2)}) copy-start(bf16[128,128]{1,0:T(8,128)(2,1)} %get-tuple-element.8) | copy-start | bytes 98308

commit v3 on v2

--- a/solution.py
+++ b/solution.py
@@ -13,22 +13,36 @@
 LINE = WINDOW // 2
 SLOTS = WINDOW + 1
 COLS = 256
-AHEAD = 8
-LAG = 3
-BACK_LAG = 3
+ROUTE = {
+    1: (-1, 0),
+    2: (-2, 0),
+    8: (-8, 0),
+    3: (-1, 2),
+    4: (-2, 2),
+    7: (1, 8),
+    6: (2, 8),
+    5: (3, 8),
+}
+REACH = (1, 2, 3, 8)
+HUBS = (8, 2, 1)
+BACK = (("other", 4), ("other", 3), ("other", 6), ("other", 5), ("other", 7))
+BACK += (("other", 2), ("line", 4), ("line", 3), ("line", 6), ("line", 5))
+BACK += (("line", 7), ("other", 8), ("other", 1), ("line", 8), ("line", 2))
+BACK += (("line", 1), ("own", 0))
 LOW = -1e30
 HIGH = 3e38
 
 
-def nearest(n):
-    n = n + 1
-    half = n // 2
-    k = half + (n % 2) * (LINE - 2 * half)
-    return jnp.where(k == 0, LINE, k)
-
-
-def farthest(n):
-    return nearest(LINE - 1 - n)
+def choose(n, values):
+    out = values[0]
+    for j in range(1, len(values)):
+        out = jnp.where(n == j, values[j], out)
+    return out
+
+
+def at_step(n, actions):
+    for j, one in actions.items():
+        pl.when(n == j)(one)
 
 
 def kernel(
@@ -64,7 +78,7 @@
     out_buf,
     from_pair,
     from_line,
-    own_part,
+    parts,
     near,
     dq_send,
     dq_recv,
@@ -72,12 +86,13 @@
     line_recv,
     pair_send,
     pair_recv,
+    back_line_send,
+    back_line_recv,
     back_pair_send,
     back_pair_recv,
-    back_line_send,
-    back_line_recv,
     core_send,
     core_recv,
+    load_sem,
 ):
     rows = heads * blk
     tiles = rows // COLS
@@ -98,11 +113,8 @@
             "inner": (chip_at % per_group) * 2 + core_at,
         }
 
-    def later(k):
-        return device((chip + 2 * k) % chips, core)
-
-    def earlier(k):
-        return device((chip - 2 * k + chips) % chips, core)
+    def unit(k):
+        return device((chip + 2 * k + chips) % chips, core)
 
     other_core = device(chip, 1 - core)
     pair = device(chip + 1 - 2 * odd, core)
@@ -117,48 +129,38 @@
             device_id_type=MESH,
         )
 
+    def other(k):
+        return 2 * k - 1 + 2 * odd if k < LINE else 2 * LINE - 1 - (2 * LINE - 2) * odd
+
     def line_copy(k):
+        step, held = ROUTE[k]
         return copy(
-            kv.at[0], kv.at[2 * k], line_send.at[k], line_recv.at[k], later(k)
-        )
-
-    def pair_copy(m):
-        b = m + 1 - odd
+            kv.at[2 * held], kv.at[2 * k], line_send.at[k], line_recv.at[k], unit(-step)
+        )
+
+    def pair_copy(k):
+        src = 2 * k if k < LINE else 2 * LINE * odd
+        dst = 2 * k + 1 - 2 * odd if k < LINE else 1 + (2 * LINE - 2) * odd
         return copy(
-            kv.at[2 * m], kv.at[2 * b - 1], pair_send.at[b], pair_recv.at[b], pair
-        )
-
-    def pair_arrival(b):
+            kv.at[src], kv.at[dst], pair_send.at[k], pair_recv.at[k], pair
+        )
+
+    def pair_arrival(k):
         return copy(
-            kv.at[0], kv.at[2 * b - 1], pair_send.at[b], pair_recv.at[b], pair
-        )
-
-    def back_pair_copy(b):
-        m = b - odd
+            kv.at[0], kv.at[other(k)], pair_send.at[k], pair_recv.at[k], pair
+        )
+
+    def back_pair_copy(k):
         return copy(
-            out_buf.at[2 * b - 1],
-            from_pair.at[m],
-            back_pair_send.at[m],
-            back_pair_recv.at[m],
-            pair,
-        )
-
-    def back_pair_arrival(m):
+            out_buf.at[other(k)], from_pair.at[k], back_pair_send.at[k],
+            back_pair_recv.at[k], pair,
+        )
+
+    def back_line_copy(k):
+        step, held = ROUTE[k]
         return copy(
-            out_buf.at[0],
-            from_pair.at[m],
-            back_pair_send.at[m],
-            back_pair_recv.at[m],
-            pair,
-        )
-
-    def back_line_copy(k):
-        return copy(
-            out_buf.at[2 * k],
-            from_line.at[k],
-            back_line_send.at[k],
-            back_line_recv.at[k],
-            earlier(k),
+            out_buf.at[2 * k], from_line.at[k], back_line_send.at[k],
+            back_line_recv.at[k], unit(step),
         )
 
     def core_copies():
@@ -188,35 +190,45 @@
         )
 
     barrier = pltpu.get_barrier_semaphore()
-    for k in range(1, LINE + 1):
-        for to in (later(k), earlier(k)):
+    for k in REACH:
+        for to in (unit(k), unit(-k)):
             pl.semaphore_signal(barrier, inc=1, device_id=to, device_id_type=MESH)
     for to in (other_core, pair):
         pl.semaphore_signal(barrier, inc=1, device_id=to, device_id_type=MESH)
 
-    kv[0, :, :width] = k_ref[...]
-    kv[0, :, width:] = v_ref[...]
+    loads = [
+        pltpu.make_async_copy(k_ref, kv.at[0, :, pl.ds(0, width)], load_sem.at[0]),
+        pltpu.make_async_copy(v_ref, kv.at[0, :, pl.ds(width, width)], load_sem.at[1]),
+    ]
     for h in range(heads):
         at = pl.ds(pl.multiple_of(core * rows + h * blk, blk), blk)
-        rows_q[at, :] = q_ref[:, h * width : (h + 1) * width]
-        rows_do[at, :] = do_ref[:, h * width : (h + 1) * width]
+        of = pl.ds(h * width, width)
+        for j, (src, dst) in enumerate(((q_ref, rows_q), (do_ref, rows_do))):
+            loads.append(
+                pltpu.make_async_copy(
+                    src.at[:, of], dst.at[at], load_sem.at[2 + 2 * h + j]
+                )
+            )
+    for c in loads:
+        c.start()
     run_max[...] = jnp.full(run_max.shape, LOW, jnp.float32)
     run_sum[...] = jnp.zeros(run_sum.shape, jnp.float32)
     run_dot[...] = jnp.zeros(run_dot.shape, jnp.float32)
 
-    pl.semaphore_wait(barrier, 2 * LINE + 2)
-
-    def start_line(n, carry):
-        line_copy(nearest(n)).start()
-        return carry
-
+    pl.semaphore_wait(barrier, 2 * len(REACH) + 2)
+
+    def on_even(run):
+        pl.when(odd == 0)(run)
+
+    for c in loads[:2]:
+        c.wait()
+    for k in (2, 8, 1):
+        line_copy(k).start()
+    on_even(lambda: pair_copy(LINE).start())
+    for c in loads[2:]:
+        c.wait()
     for c in core_copies():
         c.start()
-    lax.fori_loop(0, AHEAD, start_line, 0)
-
-    @pl.when(odd == 0)
-    def _():
-        pair_copy(0).start()
 
     def columns(base):
         def one(i, carry):
@@ -231,6 +243,19 @@
     for c in core_arrivals():
         c.wait_recv()
     columns((1 - core) * rows)
+
+    def pass_on(k):
+        line_copy(k).wait_recv()
+        for far, (step, held) in ROUTE.items():
+            if held == k:
+                line_copy(far).start()
+        if k < LINE:
+            pair_copy(k).start()
+        else:
+            pl.when(odd == 1)(lambda: pair_copy(k).start())
+
+    for k in (8, 2, 1):
+        pass_on(k)
 
     def forward(slot, own):
         key_chip = (chip - slot + chips) % chips
@@ -274,32 +299,28 @@
 
     forward(0, True)
 
+    def take(*ks):
+        def run():
+            for k in ks:
+                pass_on(k)
+
+        return run
+
+    def arrived(k):
+        return lambda: pair_arrival(k).wait_recv()
+
+    order = (16, 4, 2, 14, 6, 12, 8, 10, other(8), other(1), other(2), other(7))
+    order += (other(3), other(6), other(4), other(5))
+    before = {3: take(7), 4: take(3), 5: take(6, 4, 5)}
+    for j, k in ((8, 8), (9, 1), (10, 2), (11, 7), (12, 3), (13, 6), (14, 4), (15, 5)):
+        before[j] = arrived(k)
+
     def gather_step(n, carry):
-        @pl.when(n < LINE)
-        def _():
-            k = nearest(n)
-            line_copy(k).wait_recv()
-
-            @pl.when(n + AHEAD < LINE)
-            def _():
-                line_copy(nearest(n + AHEAD)).start()
-
-            @pl.when((k < LINE) | (odd == 1))
-            def _():
-                pair_copy(k).start()
-
-            forward(2 * k, False)
-
-        @pl.when(n >= LAG)
-        def _():
-            k = nearest(n - LAG)
-            b = jnp.where(odd == 1, k % LINE + 1, k)
-            pair_arrival(b).wait_recv()
-            forward(2 * b - 1, False)
-
+        at_step(n, before)
+        forward(choose(n, order), False)
         return carry
 
-    lax.fori_loop(0, LINE + LAG, gather_step, 0)
+    lax.fori_loop(0, len(order), gather_step, 0)
 
     m8 = run_max[...]
     m1 = jnp.max(m8, axis=0, keepdims=True)
@@ -343,45 +364,69 @@
         )
         return dk * scale, dv
 
-    @pl.when(odd == 0)
-    def _():
-        from_pair[LINE] = jnp.zeros(from_pair.shape[1:], jnp.bfloat16)
-
-    @pl.when(odd == 1)
-    def _():
-        from_pair[0] = jnp.zeros(from_pair.shape[1:], jnp.bfloat16)
+    from_pair[0] = jnp.zeros(from_pair.shape[1:], jnp.bfloat16)
+
+    def back_arrived(k):
+        return lambda: back_pair_copy(k).wait_recv()
+
+    def starts(copy_of, k):
+        return lambda: copy_of(k).start()
+
+    back_order = []
+    back_add = []
+    back_part = []
+    back_before = {}
+    back_after = {}
+    for j, (kind, k) in enumerate(BACK):
+        back_order.append(other(k) if kind == "other" else 2 * k)
+        back_add.append(0)
+        back_part.append(len(HUBS) + 1)
+        if kind == "other":
+            back_after[j] = starts(back_pair_copy, k)
+        elif kind == "own":
+            back_part[j] = 0
+        elif k in HUBS:
+            back_part[j] = 1 + HUBS.index(k)
+        else:
+            back_add[j] = k
+            back_before[j] = back_arrived(k)
+            back_after[j] = starts(back_line_copy, k)
 
     def return_step(n, carry):
-        @pl.when(n < LINE)
-        def _():
-            k = farthest(n)
-            b = jnp.where(odd == 1, k % LINE + 1, k)
-            dk, dv = backward(2 * b - 1)
-            out_buf[2 * b - 1, :, :width] = dk.astype(jnp.bfloat16)
-            out_buf[2 * b - 1, :, width:] = dv.astype(jnp.bfloat16)
-            back_pair_copy(b).start()
-
-        @pl.when(n >= BACK_LAG)
-        def _():
-            k = farthest(n - BACK_LAG)
-            dk, dv = backward(2 * k)
-
-            @pl.when((k < LINE) | (odd == 1))
-            def _():
-                back_pair_arrival(k).wait_recv()
-
-            got = from_pair[k].astype(jnp.float32)
-            out_buf[2 * k, :, :width] = (dk + got[:, :width]).astype(jnp.bfloat16)
-            out_buf[2 * k, :, width:] = (dv + got[:, width:]).astype(jnp.bfloat16)
-            back_line_copy(k).start()
-
+        slot = choose(n, back_order)
+        dk, dv = backward(slot)
+        at_step(n, back_before)
+        got = from_pair[choose(n, back_add)].astype(jnp.float32)
+        part = choose(n, back_part)
+        dk = dk + got[:, :width]
+        dv = dv + got[:, width:]
+        parts[part, :, :width] = dk
+        parts[part, :, width:] = dv
+        out_buf[slot, :, :width] = dk.astype(jnp.bfloat16)
+        out_buf[slot, :, width:] = dv.astype(jnp.bfloat16)
+        at_step(n, back_after)
         return carry
 
-    lax.fori_loop(0, LINE + BACK_LAG, return_step, 0)
-
-    dk, dv = backward(0)
-    own_part[:, :width] = dk
-    own_part[:, width:] = dv
+    lax.fori_loop(0, len(BACK), return_step, 0)
+
+    def finish_hub(k):
+        at = 1 + HUBS.index(k)
+
+        def add_pair():
+            back_pair_copy(k).wait_recv()
+            parts[at] += from_pair[k].astype(jnp.float32)
+
+        if k < LINE:
+            add_pair()
+        else:
+            pl.when(odd == 1)(add_pair)
+        total = parts[at]
+        for m, (step, held) in ROUTE.items():
+            if held == k:
+                back_line_copy(m).wait_recv()
+                total = total + from_line[m].astype(jnp.float32)
+        out_buf[2 * k] = total.astype(jnp.bfloat16)
+        back_line_copy(k).start()
 
     def query_tile(i):
         at = pl.ds(pl.multiple_of(i * COLS, COLS), COLS)
@@ -400,6 +445,8 @@
     lax.fori_loop(0, tiles, far_rows, 0)
     dq_copy = copy(dq_send, dq_recv, core_send.at[3], core_recv.at[3], other_core)
     dq_copy.start()
+    for k in HUBS:
+        finish_hub(k)
 
     def near_rows(i, carry):
         part = query_tile(core * tiles + i)
@@ -414,31 +461,29 @@
 
     @pl.when(odd == 0)
     def _():
-        back_pair_arrival(0).wait_recv()
-
-    own_part[...] += from_pair[0].astype(jnp.float32)
-
-    def add_line(n, carry):
-        k = farthest(n)
+        back_pair_copy(LINE).wait_recv()
+        parts[0] += from_pair[LINE].astype(jnp.float32)
+
+    total = parts[0]
+    for k in (1, 8, 2):
         back_line_copy(k).wait_recv()
-        own_part[...] += from_line[k].astype(jnp.float32)
-        return carry
-
-    lax.fori_loop(0, LINE, add_line, 0)
-    dk_ref[...] = own_part[:, :width].astype(jnp.bfloat16)
-    dv_ref[...] = own_part[:, width:].astype(jnp.bfloat16)
-
-    def finish(n, carry):
-        k = n + 1
+        total = total + from_line[k].astype(jnp.float32)
+    dk_ref[...] = total[:, :width].astype(jnp.bfloat16)
+    dv_ref[...] = total[:, width:].astype(jnp.bfloat16)
+
+    for k in range(1, LINE + 1):
         line_copy(k).wait_send()
         back_line_copy(k).wait_send()
-        pair_copy(n + odd).wait_send()
+        pair_copy(k).wait_send()
         back_pair_copy(k).wait_send()
-        return carry
-
-    lax.fori_loop(0, LINE, finish, 0)
     for c in core_copies():
         c.wait_send()
+
+
+def hand_out(dq_ref, dk_ref, dv_ref, dq_out, dk_out, dv_out):
+    dq_out[...] = dq_ref[...]
+    dk_out[...] = dk_ref[...]
+    dv_out[...] = dv_ref[...]
 
 
 def solution(mesh):
@@ -452,7 +497,7 @@
         bf16, f32 = jnp.bfloat16, jnp.float32
         vmem = pl.BlockSpec(memory_space=pltpu.VMEM)
         dma = pltpu.SemaphoreType.DMA
-        return pl.pallas_call(
+        grads = pl.pallas_call(
             functools.partial(kernel, inner_count, devices // 2, blk, width, heads),
             name="attention_backward",
             out_shape=(
@@ -460,7 +505,7 @@
                 jax.ShapeDtypeStruct(key_rows.shape, bf16),
                 jax.ShapeDtypeStruct(value_rows.shape, bf16),
             ),
-            in_specs=[vmem] * 4 + [pl.BlockSpec(memory_space=pltpu.SMEM)],
+            in_specs=[pl.BlockSpec(memory_space=pl.ANY)] * 4 + [pl.BlockSpec(memory_space=pltpu.SMEM)],
             out_specs=(vmem, vmem, vmem),
             scratch_shapes=[
                 pltpu.VMEM((SLOTS, blk, 2 * width), bf16),
@@ -482,7 +527,7 @@
                 pltpu.VMEM((SLOTS, blk, 2 * width), bf16),
                 pltpu.VMEM((LINE + 1, blk, 2 * width), bf16),
                 pltpu.VMEM((LINE + 1, blk, 2 * width), bf16),
-                pltpu.VMEM((blk, 2 * width), f32),
+                pltpu.VMEM((len(HUBS) + 2, blk, 2 * width), f32),
                 pltpu.VMEM((blk, heads * width), f32),
                 pltpu.VMEM((blk, heads * width), bf16),
                 pltpu.VMEM((blk, heads * width), bf16),
@@ -496,11 +541,19 @@
                 dma((LINE + 1,)),
                 dma((4,)),
                 dma((4,)),
+                dma((2 + 2 * heads,)),
             ],
             compiler_params=pltpu.CompilerParams(
-                collective_id=0, has_side_effects=True, vmem_limit_bytes=60 << 20
+                collective_id=0, has_side_effects=True, vmem_limit_bytes=56 << 20
             ),
         )(queries, key_rows, value_rows, grad_output, doc_blocks)
+        return pl.pallas_call(
+            hand_out,
+            name="hand_out",
+            out_shape=[jax.ShapeDtypeStruct(x.shape, x.dtype) for x in grads],
+            in_specs=[vmem] * 3,
+            out_specs=[vmem] * 3,
+        )(*grads)
 
     rows = P(("outer", "inner"), None)
     return jax.shard_map(

time: 65.5 us -> 62.6 us (0.956)
  local copies, waits for them, and re-layouts: 3.06 us -> 0 us
    unnamed x7 -> x0, local copies, waits for them, and re-layouts: 3.06 us -> none
    pallas_call x1, Pallas kernels: 61.6 us -> 59.7 us  [shards(): pl.pallas_call(functools.partial(kernel, inner_count, devices // 2, blk,...]
    pallas_call x0 -> x1, Pallas kernels: none -> 1.7 us  [shards(): pl.pallas_call(hand_out, name='hand_out', out_shape=[jax.ShapeDtypeStruct...]
where the time goes in v3:
time: 62.6 us; the launch traced here: 62 us
  Pallas kernels  61.4 us (98%)
  between operations  0.64 us (1%)
    pallas_call x1, Pallas kernels, shards(): pl.pallas_call(functools.partial(kernel, inner_count, devices // 2, blk,...  59.7 us
    pallas_call x1, Pallas kernels, shards(): pl.pallas_call(hand_out, name='hand_out', out_shape=[jax.ShapeDtypeStruct...  1.7 us

profile of v3, /device:TPU:1, one launch (start us, length us, event | category | flops | bytes accessed | tf_op | source)
XLA Modules:
  0.0 62.0 jit_solution(12019415164751629802)
XLA Ops:
  0.6 59.7 %attention_backward.1 = (bf16[128,1024]{1,0:T(8,128)(2,1)}, bf16[128,128]{1,0:T(8,128)(2,1)}, bf16[128,128]{1,0:T(8,128)(2,1)}) custom-call(bf16[128,1024]{1,0:T(8,128)(2,1)} %q_ref.1, bf16[128,128]{1,0:T(8,128)(2,1)} %k_ref.1, bf16[128,128]{1,0:T(8,128)(2,1)} %v_ref.1, bf16[128,1024]{1,0:T(8,128)(2,1)} %do_ref.1, s32[256]{0:T(256)} %doc_ref.1), custom_call_target="tpu_custom_call" | custom-call | tf_op jit(solution)/shard_map/attention_backward/pallas_call | solution.py:500
  60.4 1.7 %hand_out.1 = (bf16[128,1024]{1,0:T(8,128)(2,1)}, bf16[128,128]{1,0:T(8,128)(2,1)}, bf16[128,128]{1,0:T(8,128)(2,1)}) custom-call(bf16[128,1024]{1,0:T(8,128)(2,1)} %get-tuple-element.6.dq_ref, bf16[128,128]{1,0:T(8,128)(2,1)} %get-tuple-element.7.dk_ref, bf16[128,128]{1,0:T(8,128)(2,1)} %get-tuple-element.8.dv_ref), custom_call_target="tpu_custom_call" | custom-call | tf_op jit(solution)/shard_map/hand_out/pallas_call | solution.py:550

commit v4 on v3

--- a/solution.py
+++ b/solution.py
@@ -17,17 +17,17 @@
     1: (-1, 0),
     2: (-2, 0),
     8: (-8, 0),
+    6: (-6, 0),
     3: (-1, 2),
     4: (-2, 2),
     7: (1, 8),
-    6: (2, 8),
-    5: (3, 8),
+    5: (1, 6),
 }
-REACH = (1, 2, 3, 8)
-HUBS = (8, 2, 1)
-BACK = (("other", 4), ("other", 3), ("other", 6), ("other", 5), ("other", 7))
-BACK += (("other", 2), ("line", 4), ("line", 3), ("line", 6), ("line", 5))
-BACK += (("line", 7), ("other", 8), ("other", 1), ("line", 8), ("line", 2))
+REACH = (1, 2, 6, 8)
+HUBS = (6, 8, 2, 1)
+BACK = (("other", 4), ("other", 5), ("other", 3), ("other", 7), ("other", 6))
+BACK += (("other", 2), ("line", 4), ("line", 5), ("line", 3), ("line", 7))
+BACK += (("other", 8), ("other", 1), ("line", 6), ("line", 2), ("line", 8))
 BACK += (("line", 1), ("own", 0))
 LOW = -1e30
 HIGH = 3e38
@@ -222,7 +222,7 @@
 
     for c in loads[:2]:
         c.wait()
-    for k in (2, 8, 1):
+    for k in (6, 2, 8, 1):
         line_copy(k).start()
     on_even(lambda: pair_copy(LINE).start())
     for c in loads[2:]:
@@ -309,10 +309,10 @@
     def arrived(k):
         return lambda: pair_arrival(k).wait_recv()
 
-    order = (16, 4, 2, 14, 6, 12, 8, 10, other(8), other(1), other(2), other(7))
-    order += (other(3), other(6), other(4), other(5))
-    before = {3: take(7), 4: take(3), 5: take(6, 4, 5)}
-    for j, k in ((8, 8), (9, 1), (10, 2), (11, 7), (12, 3), (13, 6), (14, 4), (15, 5)):
+    order = (16, 4, 12, 2, 14, 6, 10, 8, other(8), other(2), other(1), other(6))
+    order += (other(7), other(3), other(5), other(4))
+    before = {2: take(6), 4: take(7), 5: take(3), 6: take(5, 4)}
+    for j, k in ((8, 8), (9, 2), (10, 1), (11, 6), (12, 7), (13, 3), (14, 5), (15, 4)):
         before[j] = arrived(k)
 
     def gather_step(n, carry):
@@ -428,6 +428,8 @@
         out_buf[2 * k] = total.astype(jnp.bfloat16)
         back_line_copy(k).start()
 
+    finish_hub(HUBS[0])
+
     def query_tile(i):
         at = pl.ds(pl.multiple_of(i * COLS, COLS), COLS)
         part = jnp.dot(keys_t[...], dsc[:, at], preferred_element_type=jnp.float32)
@@ -445,7 +447,7 @@
     lax.fori_loop(0, tiles, far_rows, 0)
     dq_copy = copy(dq_send, dq_recv, core_send.at[3], core_recv.at[3], other_core)
     dq_copy.start()
-    for k in HUBS:
+    for k in HUBS[1:]:
         finish_hub(k)
 
     def near_rows(i, carry):
@@ -465,7 +467,7 @@
         parts[0] += from_pair[LINE].astype(jnp.float32)
 
     total = parts[0]
-    for k in (1, 8, 2):
+    for k in (1, 8, 2, 6):
         back_line_copy(k).wait_recv()
         total = total + from_line[k].astype(jnp.float32)
     dk_ref[...] = total[:, :width].astype(jnp.bfloat16)

time: 62.6 us -> 59.1 us (0.944)
  Pallas kernels: 61.4 us -> 58.4 us
    pallas_call x1, Pallas kernels: 59.7 us -> 56.7 us  [shards(): pl.pallas_call(functools.partial(kernel, inner_count, devices // 2, blk,...]
where the time goes in v4:
time: 59.1 us; the launch traced here: 59 us
  Pallas kernels  58.4 us (99%)
  between operations  0.64 us (1%)
    pallas_call x1, Pallas kernels, shards(): pl.pallas_call(functools.partial(kernel, inner_count, devices // 2, blk,...  56.7 us
    pallas_call x1, Pallas kernels, shards(): pl.pallas_call(hand_out, name='hand_out', out_shape=[jax.ShapeDtypeStruct...  1.7 us

profile of v4, /device:TPU:1, one launch (start us, length us, event | category | flops | bytes accessed | tf_op | source)
XLA Modules:
  0.0 59.0 jit_solution(13776519646535308496)
XLA Ops:
  0.6 56.7 %attention_backward.1 = (bf16[128,1024]{1,0:T(8,128)(2,1)}, bf16[128,128]{1,0:T(8,128)(2,1)}, bf16[128,128]{1,0:T(8,128)(2,1)}) custom-call(bf16[128,1024]{1,0:T(8,128)(2,1)} %q_ref.1, bf16[128,128]{1,0:T(8,128)(2,1)} %k_ref.1, bf16[128,128]{1,0:T(8,128)(2,1)} %v_ref.1, bf16[128,1024]{1,0:T(8,128)(2,1)} %do_ref.1, s32[256]{0:T(256)} %doc_ref.1), custom_call_target="tpu_custom_call" | custom-call | tf_op jit(solution)/shard_map/attention_backward/pallas_call | solution.py:502
  57.3 1.7 %hand_out.1 = (bf16[128,1024]{1,0:T(8,128)(2,1)}, bf16[128,128]{1,0:T(8,128)(2,1)}, bf16[128,128]{1,0:T(8,128)(2,1)}) custom-call(bf16[128,1024]{1,0:T(8,128)(2,1)} %get-tuple-element.6.dq_ref, bf16[128,128]{1,0:T(8,128)(2,1)} %get-tuple-element.7.dk_ref, bf16[128,128]{1,0:T(8,128)(2,1)} %get-tuple-element.8.dv_ref), custom_call_target="tpu_custom_call" | custom-call | tf_op jit(solution)/shard_map/hand_out/pallas_call | solution.py:552

commit v5 on v4

--- a/solution.py
+++ b/solution.py
@@ -18,15 +18,15 @@
     2: (-2, 0),
     8: (-8, 0),
     6: (-6, 0),
+    4: (-2, 2),
     3: (-1, 2),
-    4: (-2, 2),
     7: (1, 8),
     5: (1, 6),
 }
 REACH = (1, 2, 6, 8)
-HUBS = (6, 8, 2, 1)
-BACK = (("other", 4), ("other", 5), ("other", 3), ("other", 7), ("other", 6))
-BACK += (("other", 2), ("line", 4), ("line", 5), ("line", 3), ("line", 7))
+HUBS = (6, 2, 8, 1)
+BACK = (("other", 5), ("other", 4), ("other", 7), ("other", 3), ("other", 6))
+BACK += (("other", 2), ("line", 5), ("line", 4), ("line", 7), ("line", 3))
 BACK += (("other", 8), ("other", 1), ("line", 6), ("line", 2), ("line", 8))
 BACK += (("line", 1), ("own", 0))
 LOW = -1e30
@@ -240,9 +240,6 @@
         lax.fori_loop(0, heads, one, 0)
 
     columns(core * rows)
-    for c in core_arrivals():
-        c.wait_recv()
-    columns((1 - core) * rows)
 
     def pass_on(k):
         line_copy(k).wait_recv()
@@ -254,8 +251,13 @@
         else:
             pl.when(odd == 1)(lambda: pair_copy(k).start())
 
-    for k in (8, 2, 1):
-        pass_on(k)
+    pass_on(8)
+    pass_on(2)
+    for c in core_arrivals():
+        c.wait_recv()
+    columns((1 - core) * rows)
+    pass_on(1)
+    pass_on(6)
 
     def forward(slot, own):
         key_chip = (chip - slot + chips) % chips
@@ -311,7 +313,7 @@
 
     order = (16, 4, 12, 2, 14, 6, 10, 8, other(8), other(2), other(1), other(6))
     order += (other(7), other(3), other(5), other(4))
-    before = {2: take(6), 4: take(7), 5: take(3), 6: take(5, 4)}
+    before = {4: take(7), 5: take(3), 6: take(5, 4)}
     for j, k in ((8, 8), (9, 2), (10, 1), (11, 6), (12, 7), (13, 3), (14, 5), (15, 4)):
         before[j] = arrived(k)
 

time: 59.1 us -> 59.5 us (level)
  no operation moved by 1% of the time
where the time goes in v5:
time: 59.5 us; the launch traced here: 58.9 us
  Pallas kernels  58.3 us (98%)
  between operations  0.64 us (1%)
    pallas_call x1, Pallas kernels, shards(): pl.pallas_call(functools.partial(kernel, inner_count, devices // 2, blk,...  56.6 us
    pallas_call x1, Pallas kernels, shards(): pl.pallas_call(hand_out, name='hand_out', out_shape=[jax.ShapeDtypeStruct...  1.7 us

profile of v5, /device:TPU:1, one launch (start us, length us, event | category | flops | bytes accessed | tf_op | source)
XLA Modules:
  0.0 58.9 jit_solution(15275242295471124118)
XLA Ops:
  0.6 56.6 %attention_backward.1 = (bf16[128,1024]{1,0:T(8,128)(2,1)}, bf16[128,128]{1,0:T(8,128)(2,1)}, bf16[128,128]{1,0:T(8,128)(2,1)}) custom-call(bf16[128,1024]{1,0:T(8,128)(2,1)} %q_ref.1, bf16[128,128]{1,0:T(8,128)(2,1)} %k_ref.1, bf16[128,128]{1,0:T(8,128)(2,1)} %v_ref.1, bf16[128,1024]{1,0:T(8,128)(2,1)} %do_ref.1, s32[256]{0:T(256)} %doc_ref.1), custom_call_target="tpu_custom_call" | custom-call | tf_op jit(solution)/shard_map/attention_backward/pallas_call | solution.py:504
  57.2 1.7 %hand_out.1 = (bf16[128,1024]{1,0:T(8,128)(2,1)}, bf16[128,128]{1,0:T(8,128)(2,1)}, bf16[128,128]{1,0:T(8,128)(2,1)}) custom-call(bf16[128,1024]{1,0:T(8,128)(2,1)} %get-tuple-element.6.dq_ref, bf16[128,128]{1,0:T(8,128)(2,1)} %get-tuple-element.7.dk_ref, bf16[128,128]{1,0:T(8,128)(2,1)} %get-tuple-element.8.dv_ref), custom_call_target="tpu_custom_call" | custom-call | tf_op jit(solution)/shard_map/hand_out/pallas_call | solution.py:554
